TPU v7x, 256 devices: a whole 4x4x8 slice. The times are simulated.
256 devices in a mesh: blk: 64 (over y_hi, z, x), rep: 2 (over core), layer: 2 (over y_lo).
Axes of the slice: x: 4, y: 4 (y_hi: 2, y_lo: 2; y = y_hi * 2 + y_lo), z: 8, core: 2. Of those that a mesh axis runs over, the one named last changes fastest.
Arguments:
- features: bfloat16 [3, 49152, 512], P(None, 'blk', 'rep'), may hold values from -6 to 6
- weights: bfloat16 [2, 512, 512], P('layer', None, 'rep'), may hold values from -0.25 to 0.25
- biases: bfloat16 [2, 512], P('layer', 'rep'), may hold values from -3 to 3
- tile_vals: bfloat16 [384, 24, 128, 128], P('blk'), may hold values from -0.25 to 0.25
- tile_cols: int32 [384, 24], P('blk'), may hold values from 0 to 383, as said below
- tile_counts: int32 [384], P('blk'), may hold values from 1 to 24, as said below
Outputs:
- layer_outputs: bfloat16 [2, 3, 49152, 512], P('layer', None, 'blk', 'rep')
Inputs may be any that keep to these rules, and one draw needn't show every extreme that they name: tile_cols[b, k] is a column block of a blk index at most 2 places from the index that holds row block b, counted around the closed loop of blk indices: (b // 6 + d) mod (the number of blk indices), times 6, plus j, with -2 <= d <= 2 and 0 <= j < 6; the 24 entries of one row are distinct. The live tiles of row block b are its slots 0 to tile_counts[b] - 1; some row block has all 24 live.
All inputs are finite; a program needn't handle non-finite values.
Results may differ from a plain program's by a relative error of at most 0.0055.
Values may be sent and summed in bfloat16 or wider, within the bound.
A program may use at most 64 MiB of HBM per device.

v0:
```python
import jax
import jax.numpy as jnp
from jax import lax
from jax.sharding import PartitionSpec as P

BLOCK = 128
REACH = 2


def shifted(value, axis, by):
    devices = lax.axis_size(axis)
    return lax.ppermute(value, axis, [(i, (i + by) % devices) for i in range(devices)])


def shifted_2(value, axis, by):
    devices = lax.axis_size(axis)
    pairs = [(i, i + by) for i in range(devices) if 0 <= i + by < devices]
    return lax.ppermute(value, axis, pairs)


def transform(inputs, weight_cols):
    running = jnp.dot(
        lax.all_gather(inputs, "rep", axis=1, tiled=True),
        weight_cols,
        preferred_element_type=jnp.float32,
    )
    return running.astype(jnp.bfloat16)


def window(transformed):
    moving = shifted(transformed, "blk", -REACH)
    window_slabs = [moving]
    for offset in range(2 * REACH):
        moving = shifted(moving, "blk", 1)
        window_slabs.append(moving)
    window_slabs = window_slabs[::-1]
    stacked = jnp.concatenate(window_slabs, axis=0)
    return stacked.reshape(-1, BLOCK, transformed.shape[1])


def tile_products(blocks, values, columns, live):
    picked = blocks[columns]
    picked = jnp.where(live[:, :, None, None], picked, jnp.zeros((), jnp.bfloat16))
    return jnp.einsum("btij,btjf->bif", values, picked, preferred_element_type=jnp.float32)


def aggregate(blocks, tile_vals, local_cols, live_mask):
    return tile_products(blocks, tile_vals, local_cols, live_mask)


def per_device(features, weights, biases, tile_vals, tile_cols, tile_counts):
    segment_index = lax.axis_index("layer")
    block_index = lax.axis_index("blk")
    cycle_length = lax.axis_size("blk")
    row_blocks = tile_cols.shape[0]
    local_cols = (
        tile_cols // row_blocks - block_index + REACH
    ) % cycle_length * row_blocks + tile_cols % row_blocks
    slot_ids = lax.broadcasted_iota(jnp.int32, tile_cols.shape, 1)
    live_mask = slot_ids < tile_counts[:, None]
    snapshots = features.shape[0]
    weight_cols = weights[0]
    bias_row = biases[0].astype(jnp.float32)
    received = jnp.zeros_like(features[0])
    first_outputs = []
    second_outputs = []
    for tick_index in range(snapshots + 1):
        own_input = features[min(tick_index, snapshots - 1)]
        inputs = jnp.where(segment_index == 0, own_input, received)
        transformed = transform(inputs, weight_cols)
        blocks = window(transformed)
        summed = aggregate(blocks, tile_vals, local_cols, live_mask)
        summed = summed.reshape(inputs.shape[0], -1) + bias_row
        rectified = jnp.where(segment_index == 0, jnp.maximum(summed, 0.0), summed)
        produced = rectified.astype(jnp.bfloat16)
        if tick_index < snapshots:
            first_outputs.append(produced)
            received = shifted_2(produced, "layer", 1)
        if tick_index >= 1:
            second_outputs.append(produced)
    result = jnp.where(segment_index == 0, jnp.stack(first_outputs), jnp.stack(second_outputs))
    return result[None]


def solution(mesh):
    return jax.shard_map(
        per_device,
        mesh=mesh,
        in_specs=(
            P(None, "blk", "rep"),
            P("layer", None, "rep"),
            P("layer", "rep"),
            P("blk", None, None, None),
            P("blk", None),
            P("blk"),
        ),
        out_specs=P("layer", None, "blk", "rep"),
        check_vma=False,
    )
```

profile of v0, /device:TPU:8, one launch (start us, length us, event | category | flops | bytes accessed | tf_op | source)
XLA Modules:
  0.0 397.6 jit_solution(14156785914753523032)
XLA Ops:
  3.8 10.1 %collective-permute-start = (bf16[768,256]{1,0:T(8,128)(2,1)S(1)}, bf16[768,256]{1,0:T(8,128)(2,1)S(1)}, u32[]{:S(2)}, u32[]{:S(2)}) collective-permute-start(bf16[768,256]{1,0:T(8,128)(2,1)S(1)} %convolution_convert_fusion.3), channel_id=1, source_target_pairs={{0,248},{4,252},{8,0},{12,4},{16,8},{20,12},{24,16},{28,20},{32,24... | collective-permute-start | bytes 1179656 | tf_op jit(solution)/shard_map/ppermute | solution.py:12
  14.0 8.7 %collective-permute-done = bf16[768,256]{1,0:T(8,128)(2,1)S(1)} collective-permute-done((bf16[768,256]{1,0:T(8,128)(2,1)S(1)}, bf16[768,256]{1,0:T(8,128)(2,1)S(1)}, u32[]{:S(2)}, u32[]{:S(2)}) %collective-permute-start) | collective-permute-done | bytes 393248 | tf_op jit(solution)/shard_map/ppermute | solution.py:12
  23.2 16.2 %collective-permute-done.1 = bf16[768,256]{1,0:T(8,128)(2,1)S(1)} collective-permute-done((bf16[768,256]{1,0:T(8,128)(2,1)S(1)}, bf16[768,256]{1,0:T(8,128)(2,1)S(1)}, u32[]{:S(2)}, u32[]{:S(2)}) %collective-permute-start.1) | collective-permute-done | bytes 393248 | tf_op jit(solution)/shard_map/ppermute | solution.py:12
  39.4 15.4 %collective-permute-done.2 = bf16[768,256]{1,0:T(8,128)(2,1)S(1)} collective-permute-done((bf16[768,256]{1,0:T(8,128)(2,1)S(1)}, bf16[768,256]{1,0:T(8,128)(2,1)S(1)}, u32[]{:S(2)}, u32[]{:S(2)}) %collective-permute-start.2) | collective-permute-done | bytes 393248 | tf_op jit(solution)/shard_map/ppermute | solution.py:12
  54.9 14.6 %collective-permute-done.3 = bf16[768,256]{1,0:T(8,128)(2,1)S(1)} collective-permute-done((bf16[768,256]{1,0:T(8,128)(2,1)S(1)}, bf16[768,256]{1,0:T(8,128)(2,1)S(1)}, u32[]{:S(2)}, u32[]{:S(2)}) %collective-permute-start.3) | collective-permute-done | bytes 393248 | tf_op jit(solution)/shard_map/ppermute | solution.py:12
  70.2 13.1 %collective-permute-done.4 = bf16[768,256]{1,0:T(8,128)(2,1)} collective-permute-done((bf16[768,256]{1,0:T(8,128)(2,1)S(1)}, bf16[768,256]{1,0:T(8,128)(2,1)}, u32[]{:S(2)}, u32[]{:S(2)}) %collective-permute-start.4) | collective-permute-done | bytes 393248 | tf_op jit(solution)/shard_map/ppermute | solution.py:12
  85.4 7.3 %gather_fusion = bf16[144,128,256]{2,1,0:T(8,128)(2,1)} fusion(bf16[30,128,256]{2,1,0:T(8,128)(2,1)S(1)} %bitcast.80, s32[1024]{0:T(1024)S(1)} %pad_clamp_fusion), kind=kCustom, calls=%fused_computation | custom fusion | bytes 18874944 | tf_op jit(solution)/shard_map/gather | solution.py:42
  92.7 6.7 %fusion.6 = f32[6,256,128,1]{1,2,3,0:T(8,128)S(1)} fusion(bf16[6,24,128,128]{3,2,1,0:T(8,128)(2,1)} %param.9, bf16[6,24,128,256]{3,2,1,0:T(8,128)(2,1)} %bitcast.85, pred[6,24]{1,0:T(8,128)(4,1)S(1)} %iota_compare_fusion), kind=kOutput, calls=%fused_computation.10 | convolution fusion | flops 1212678144 | bytes 14942352 | tf_op jit(solution)/shard_map/btij,btjf->bif/dot_general | solution.py:44
  100.8 8.4 %collective-permute-done.5 = bf16[768,256]{1,0:T(8,128)(2,1)S(1)} collective-permute-done((bf16[768,256]{1,0:T(8,128)(2,1)S(1)}, bf16[768,256]{1,0:T(8,128)(2,1)S(1)}, u32[]{:S(2)}, u32[]{:S(2)}) %collective-permute-start.5) | collective-permute-done | bytes 393248 | tf_op jit(solution)/shard_map/ppermute | solution.py:18
  113.0 13.0 %collective-permute-done.6 = bf16[768,256]{1,0:T(8,128)(2,1)S(1)} collective-permute-done((bf16[768,256]{1,0:T(8,128)(2,1)S(1)}, bf16[768,256]{1,0:T(8,128)(2,1)S(1)}, u32[]{:S(2)}, u32[]{:S(2)}) %collective-permute-start.6) | collective-permute-done | bytes 393248 | tf_op jit(solution)/shard_map/ppermute | solution.py:12
  126.0 15.7 %collective-permute-done.7 = bf16[768,256]{1,0:T(8,128)(2,1)S(1)} collective-permute-done((bf16[768,256]{1,0:T(8,128)(2,1)S(1)}, bf16[768,256]{1,0:T(8,128)(2,1)S(1)}, u32[]{:S(2)}, u32[]{:S(2)}) %collective-permute-start.7) | collective-permute-done | bytes 393248 | tf_op jit(solution)/shard_map/ppermute | solution.py:12
  141.7 14.8 %collective-permute-done.8 = bf16[768,256]{1,0:T(8,128)(2,1)S(1)} collective-permute-done((bf16[768,256]{1,0:T(8,128)(2,1)S(1)}, bf16[768,256]{1,0:T(8,128)(2,1)S(1)}, u32[]{:S(2)}, u32[]{:S(2)}) %collective-permute-start.8) | collective-permute-done | bytes 393248 | tf_op jit(solution)/shard_map/ppermute | solution.py:12
  156.5 14.0 %collective-permute-done.9 = bf16[768,256]{1,0:T(8,128)(2,1)S(1)} collective-permute-done((bf16[768,256]{1,0:T(8,128)(2,1)S(1)}, bf16[768,256]{1,0:T(8,128)(2,1)S(1)}, u32[]{:S(2)}, u32[]{:S(2)}) %collective-permute-start.9) | collective-permute-done | bytes 393248 | tf_op jit(solution)/shard_map/ppermute | solution.py:12
  170.5 13.5 %collective-permute-done.10 = bf16[768,256]{1,0:T(8,128)(2,1)S(1)} collective-permute-done((bf16[768,256]{1,0:T(8,128)(2,1)S(1)}, bf16[768,256]{1,0:T(8,128)(2,1)S(1)}, u32[]{:S(2)}, u32[]{:S(2)}) %collective-permute-start.10) | collective-permute-done | bytes 393248 | tf_op jit(solution)/shard_map/ppermute | solution.py:12
  184.2 7.3 %gather_fusion.1 = bf16[144,128,256]{2,1,0:T(8,128)(2,1)} fusion(bf16[30,128,256]{2,1,0:T(8,128)(2,1)S(1)} %bitcast.81, s32[1024]{0:T(1024)S(1)} %pad_clamp_fusion), kind=kCustom, calls=%fused_computation.1 | custom fusion | bytes 18874944 | tf_op jit(solution)/shard_map/gather | solution.py:42
  191.5 6.7 %fusion.4 = f32[6,256,128,1]{1,2,3,0:T(8,128)S(1)} fusion(bf16[6,24,128,128]{3,2,1,0:T(8,128)(2,1)} %param.9, bf16[6,24,128,256]{3,2,1,0:T(8,128)(2,1)} %bitcast.86, pred[6,24]{1,0:T(8,128)(4,1)S(1)} %iota_compare_fusion), kind=kOutput, calls=%fused_computation.8 | convolution fusion | flops 1212678144 | bytes 14942352 | tf_op jit(solution)/shard_map/btij,btjf->bif/dot_general | solution.py:44
  199.6 8.4 %collective-permute-done.11 = bf16[768,256]{1,0:T(8,128)(2,1)S(1)} collective-permute-done((bf16[768,256]{1,0:T(8,128)(2,1)S(1)}, bf16[768,256]{1,0:T(8,128)(2,1)S(1)}, u32[]{:S(2)}, u32[]{:S(2)}) %collective-permute-start.11) | collective-permute-done | bytes 393248 | tf_op jit(solution)/shard_map/ppermute | solution.py:18
  211.8 13.0 %collective-permute-done.12 = bf16[768,256]{1,0:T(8,128)(2,1)S(1)} collective-permute-done((bf16[768,256]{1,0:T(8,128)(2,1)S(1)}, bf16[768,256]{1,0:T(8,128)(2,1)S(1)}, u32[]{:S(2)}, u32[]{:S(2)}) %collective-permute-start.12) | collective-permute-done | bytes 393248 | tf_op jit(solution)/shard_map/ppermute | solution.py:12
  224.8 15.7 %collective-permute-done.13 = bf16[768,256]{1,0:T(8,128)(2,1)S(1)} collective-permute-done((bf16[768,256]{1,0:T(8,128)(2,1)S(1)}, bf16[768,256]{1,0:T(8,128)(2,1)S(1)}, u32[]{:S(2)}, u32[]{:S(2)}) %collective-permute-start.13) | collective-permute-done | bytes 393248 | tf_op jit(solution)/shard_map/ppermute | solution.py:12
  240.5 14.9 %collective-permute-done.14 = bf16[768,256]{1,0:T(8,128)(2,1)S(1)} collective-permute-done((bf16[768,256]{1,0:T(8,128)(2,1)S(1)}, bf16[768,256]{1,0:T(8,128)(2,1)S(1)}, u32[]{:S(2)}, u32[]{:S(2)}) %collective-permute-start.14) | collective-permute-done | bytes 393248 | tf_op jit(solution)/shard_map/ppermute | solution.py:12
  255.4 14.0 %collective-permute-done.15 = bf16[768,256]{1,0:T(8,128)(2,1)S(1)} collective-permute-done((bf16[768,256]{1,0:T(8,128)(2,1)S(1)}, bf16[768,256]{1,0:T(8,128)(2,1)S(1)}, u32[]{:S(2)}, u32[]{:S(2)}) %collective-permute-start.15) | collective-permute-done | bytes 393248 | tf_op jit(solution)/shard_map/ppermute | solution.py:12
  269.4 13.5 %collective-permute-done.16 = bf16[768,256]{1,0:T(8,128)(2,1)S(1)} collective-permute-done((bf16[768,256]{1,0:T(8,128)(2,1)S(1)}, bf16[768,256]{1,0:T(8,128)(2,1)S(1)}, u32[]{:S(2)}, u32[]{:S(2)}) %collective-permute-start.16) | collective-permute-done | bytes 393248 | tf_op jit(solution)/shard_map/ppermute | solution.py:12
  283.0 7.3 %gather_fusion.2 = bf16[144,128,256]{2,1,0:T(8,128)(2,1)} fusion(bf16[30,128,256]{2,1,0:T(8,128)(2,1)S(1)} %bitcast.82, s32[1024]{0:T(1024)S(1)} %pad_clamp_fusion), kind=kCustom, calls=%fused_computation.2 | custom fusion | bytes 18874944 | tf_op jit(solution)/shard_map/gather | solution.py:42
  290.3 6.7 %fusion.2 = f32[6,256,128,1]{1,2,3,0:T(8,128)S(1)} fusion(bf16[6,24,128,128]{3,2,1,0:T(8,128)(2,1)} %param.9, bf16[6,24,128,256]{3,2,1,0:T(8,128)(2,1)} %bitcast.87, pred[6,24]{1,0:T(8,128)(4,1)S(1)} %iota_compare_fusion), kind=kOutput, calls=%fused_computation.6 | convolution fusion | flops 1212678144 | bytes 14942352 | tf_op jit(solution)/shard_map/btij,btjf->bif/dot_general | solution.py:44
  298.4 8.4 %collective-permute-done.17 = bf16[768,256]{1,0:T(8,128)(2,1)S(1)} collective-permute-done((bf16[768,256]{1,0:T(8,128)(2,1)S(1)}, bf16[768,256]{1,0:T(8,128)(2,1)S(1)}, u32[]{:S(2)}, u32[]{:S(2)}) %collective-permute-start.17) | collective-permute-done | bytes 393248 | tf_op jit(solution)/shard_map/ppermute | solution.py:18
  310.7 13.0 %collective-permute-done.18 = bf16[768,256]{1,0:T(8,128)(2,1)S(1)} collective-permute-done((bf16[768,256]{1,0:T(8,128)(2,1)S(1)}, bf16[768,256]{1,0:T(8,128)(2,1)S(1)}, u32[]{:S(2)}, u32[]{:S(2)}) %collective-permute-start.18) | collective-permute-done | bytes 393248 | tf_op jit(solution)/shard_map/ppermute | solution.py:12
  323.6 15.7 %collective-permute-done.19 = bf16[768,256]{1,0:T(8,128)(2,1)S(1)} collective-permute-done((bf16[768,256]{1,0:T(8,128)(2,1)S(1)}, bf16[768,256]{1,0:T(8,128)(2,1)S(1)}, u32[]{:S(2)}, u32[]{:S(2)}) %collective-permute-start.19) | collective-permute-done | bytes 393248 | tf_op jit(solution)/shard_map/ppermute | solution.py:12
  339.3 14.8 %collective-permute-done.20 = bf16[768,256]{1,0:T(8,128)(2,1)S(1)} collective-permute-done((bf16[768,256]{1,0:T(8,128)(2,1)S(1)}, bf16[768,256]{1,0:T(8,128)(2,1)S(1)}, u32[]{:S(2)}, u32[]{:S(2)}) %collective-permute-start.20) | collective-permute-done | bytes 393248 | tf_op jit(solution)/shard_map/ppermute | solution.py:12
  354.2 14.0 %collective-permute-done.21 = bf16[768,256]{1,0:T(8,128)(2,1)S(1)} collective-permute-done((bf16[768,256]{1,0:T(8,128)(2,1)S(1)}, bf16[768,256]{1,0:T(8,128)(2,1)S(1)}, u32[]{:S(2)}, u32[]{:S(2)}) %collective-permute-start.21) | collective-permute-done | bytes 393248 | tf_op jit(solution)/shard_map/ppermute | solution.py:12
  368.2 13.5 %collective-permute-done.22 = bf16[768,256]{1,0:T(8,128)(2,1)S(1)} collective-permute-done((bf16[768,256]{1,0:T(8,128)(2,1)S(1)}, bf16[768,256]{1,0:T(8,128)(2,1)S(1)}, u32[]{:S(2)}, u32[]{:S(2)}) %collective-permute-start.22) | collective-permute-done | bytes 393248 | tf_op jit(solution)/shard_map/ppermute | solution.py:12
  381.9 7.3 %gather_fusion.3 = bf16[144,128,256]{2,1,0:T(8,128)(2,1)} fusion(bf16[30,128,256]{2,1,0:T(8,128)(2,1)S(1)} %bitcast.83, s32[1024]{0:T(1024)S(1)} %pad_clamp_fusion), kind=kCustom, calls=%fused_computation.3 | custom fusion | bytes 18874944 | tf_op jit(solution)/shard_map/gather | solution.py:42
  389.1 6.8 %fusion = f32[6,256,128,1]{1,2,3,0:T(8,128)S(1)} fusion(bf16[6,24,128,128]{3,2,1,0:T(8,128)(2,1)} %param.9, bf16[6,24,128,256]{3,2,1,0:T(8,128)(2,1)} %bitcast.84, pred[6,24]{1,0:T(8,128)(4,1)S(1)} %iota_compare_fusion), kind=kOutput, calls=%fused_computation.4 | convolution fusion | flops 1212678144 | bytes 14942352 | tf_op jit(solution)/shard_map/btij,btjf->bif/dot_general | solution.py:44
  (82 shorter events, 25.1 us)
Async XLA Ops:
  0.0 3.5 copy-start
  0.0 69.4 %copy-start.6 = (s32[6,24]{1,0:T(8,128)S(1)}, s32[6,24]{1,0:T(8,128)}, u32[]{:S(2)}) copy-start(s32[6,24]{1,0:T(8,128)} %param.10) | copy-start | bytes 1732
  0.0 69.5 %copy-start.7 = (bf16[1,256]{1,0:T(2,128)(2,1)S(1)}, bf16[1,256]{1,0:T(2,128)(2,1)}, u32[]{:S(2)}) copy-start(bf16[1,256]{1,0:T(2,128)(2,1)} %param.8) | copy-start | bytes 1540
  0.0 69.6 %copy-start.8 = (s32[6]{0:T(128)S(1)}, s32[6]{0:T(128)}, u32[]{:S(2)}) copy-start(s32[6]{0:T(128)} %param.11) | copy-start | bytes 76
  3.8 18.8 %collective-permute-start = (bf16[768,256]{1,0:T(8,128)(2,1)S(1)}, bf16[768,256]{1,0:T(8,128)(2,1)S(1)}, u32[]{:S(2)}, u32[]{:S(2)}) collective-permute-start(bf16[768,256]{1,0:T(8,128)(2,1)S(1)} %convolution_convert_fusion.3), channel_id=1, source_target_pairs={{0,248},{4,252},{8,0},{12,4},{16,8},{20,12},{24,16},{28,20},{32,24... | collective-permute-start | bytes 1179656 | tf_op jit(solution)/shard_map/ppermute | solution.py:12
  22.6 16.8 %collective-permute-start.1 = (bf16[768,256]{1,0:T(8,128)(2,1)S(1)}, bf16[768,256]{1,0:T(8,128)(2,1)S(1)}, u32[]{:S(2)}, u32[]{:S(2)}) collective-permute-start(bf16[768,256]{1,0:T(8,128)(2,1)S(1)} %collective-permute-done), channel_id=1, source_target_pairs={{0,4},{4,8},{8,12},{12,16},{16,20},{20,24},{24,28},{28,32},{32,36}... | collective-permute-start | bytes 1179656 | tf_op jit(solution)/shard_map/ppermute | solution.py:12
  39.4 15.4 %collective-permute-start.2 = (bf16[768,256]{1,0:T(8,128)(2,1)S(1)}, bf16[768,256]{1,0:T(8,128)(2,1)S(1)}, u32[]{:S(2)}, u32[]{:S(2)}) collective-permute-start(bf16[768,256]{1,0:T(8,128)(2,1)S(1)} %collective-permute-done.1), channel_id=1, source_target_pairs={{0,4},{4,8},{8,12},{12,16},{16,20},{20,24},{24,28},{28,32},{32,36}... | collective-permute-start | bytes 1179656 | tf_op jit(solution)/shard_map/ppermute | solution.py:12
  54.9 14.6 %collective-permute-start.3 = (bf16[768,256]{1,0:T(8,128)(2,1)S(1)}, bf16[768,256]{1,0:T(8,128)(2,1)S(1)}, u32[]{:S(2)}, u32[]{:S(2)}) collective-permute-start(bf16[768,256]{1,0:T(8,128)(2,1)S(1)} %collective-permute-done.2), channel_id=1, source_target_pairs={{0,4},{4,8},{8,12},{12,16},{16,20},{20,24},{24,28},{28,32},{32,36}... | collective-permute-start | bytes 1179656 | tf_op jit(solution)/shard_map/ppermute | solution.py:12
  69.4 0.7 copy-start.5
  69.4 13.8 %collective-permute-start.4 = (bf16[768,256]{1,0:T(8,128)(2,1)S(1)}, bf16[768,256]{1,0:T(8,128)(2,1)}, u32[]{:S(2)}, u32[]{:S(2)}) collective-permute-start(bf16[768,256]{1,0:T(8,128)(2,1)S(1)} %collective-permute-done.3), channel_id=1, source_target_pairs={{0,4},{4,8},{8,12},{12,16},{16,20},{20,24},{24,28},{28,32},{32,36}... | collective-permute-start | bytes 1179656 | tf_op jit(solution)/shard_map/ppermute | solution.py:12
  99.5 9.7 %collective-permute-start.5 = (bf16[768,256]{1,0:T(8,128)(2,1)S(1)}, bf16[768,256]{1,0:T(8,128)(2,1)S(1)}, u32[]{:S(2)}, u32[]{:S(2)}) collective-permute-start(bf16[768,256]{1,0:T(8,128)(2,1)S(1)} %fusion.17), channel_id=1, source_target_pairs={{0,1},{2,3},{4,5},{6,7},{8,9},{10,11},{12,13},{14,15},{16,17},{18,... | collective-permute-start | bytes 1179656 | tf_op jit(solution)/shard_map/ppermute | solution.py:18
  112.9 13.1 %collective-permute-start.6 = (bf16[768,256]{1,0:T(8,128)(2,1)S(1)}, bf16[768,256]{1,0:T(8,128)(2,1)S(1)}, u32[]{:S(2)}, u32[]{:S(2)}) collective-permute-start(bf16[768,256]{1,0:T(8,128)(2,1)S(1)} %convolution_convert_fusion.2), channel_id=1, source_target_pairs={{0,248},{4,252},{8,0},{12,4},{16,8},{20,12},{24,16},{28,20},{32,24... | collective-permute-start | bytes 1179656 | tf_op jit(solution)/shard_map/ppermute | solution.py:12
  126.0 15.7 %collective-permute-start.7 = (bf16[768,256]{1,0:T(8,128)(2,1)S(1)}, bf16[768,256]{1,0:T(8,128)(2,1)S(1)}, u32[]{:S(2)}, u32[]{:S(2)}) collective-permute-start(bf16[768,256]{1,0:T(8,128)(2,1)S(1)} %collective-permute-done.6), channel_id=1, source_target_pairs={{0,4},{4,8},{8,12},{12,16},{16,20},{20,24},{24,28},{28,32},{32,36}... | collective-permute-start | bytes 1179656 | tf_op jit(solution)/shard_map/ppermute | solution.py:12
  141.7 14.8 %collective-permute-start.8 = (bf16[768,256]{1,0:T(8,128)(2,1)S(1)}, bf16[768,256]{1,0:T(8,128)(2,1)S(1)}, u32[]{:S(2)}, u32[]{:S(2)}) collective-permute-start(bf16[768,256]{1,0:T(8,128)(2,1)S(1)} %collective-permute-done.7), channel_id=1, source_target_pairs={{0,4},{4,8},{8,12},{12,16},{16,20},{20,24},{24,28},{28,32},{32,36}... | collective-permute-start | bytes 1179656 | tf_op jit(solution)/shard_map/ppermute | solution.py:12
  156.5 14.0 %collective-permute-start.9 = (bf16[768,256]{1,0:T(8,128)(2,1)S(1)}, bf16[768,256]{1,0:T(8,128)(2,1)S(1)}, u32[]{:S(2)}, u32[]{:S(2)}) collective-permute-start(bf16[768,256]{1,0:T(8,128)(2,1)S(1)} %collective-permute-done.8), channel_id=1, source_target_pairs={{0,4},{4,8},{8,12},{12,16},{16,20},{20,24},{24,28},{28,32},{32,36}... | collective-permute-start | bytes 1179656 | tf_op jit(solution)/shard_map/ppermute | solution.py:12
  170.5 13.5 %collective-permute-start.10 = (bf16[768,256]{1,0:T(8,128)(2,1)S(1)}, bf16[768,256]{1,0:T(8,128)(2,1)S(1)}, u32[]{:S(2)}, u32[]{:S(2)}) collective-permute-start(bf16[768,256]{1,0:T(8,128)(2,1)S(1)} %collective-permute-done.9), channel_id=1, source_target_pairs={{0,4},{4,8},{8,12},{12,16},{16,20},{20,24},{24,28},{28,32},{32,36}... | collective-permute-start | bytes 1179656 | tf_op jit(solution)/shard_map/ppermute | solution.py:12
  198.2 13.6 %copy-start.1 = (f32[6,256,128,1]{1,2,3,0:T(8,128)}, f32[6,256,128,1]{1,2,3,0:T(8,128)S(1)}, u32[]{:S(2)}) copy-start(f32[6,256,128,1]{1,2,3,0:T(8,128)S(1)} %fusion.4) | copy-start | bytes 2359300
  198.3 9.7 %collective-permute-start.11 = (bf16[768,256]{1,0:T(8,128)(2,1)S(1)}, bf16[768,256]{1,0:T(8,128)(2,1)S(1)}, u32[]{:S(2)}, u32[]{:S(2)}) collective-permute-start(bf16[768,256]{1,0:T(8,128)(2,1)S(1)} %fusion.19), channel_id=1, source_target_pairs={{0,1},{2,3},{4,5},{6,7},{8,9},{10,11},{12,13},{14,15},{16,17},{18,... | collective-permute-start | bytes 1179656 | tf_op jit(solution)/shard_map/ppermute | solution.py:18
  211.7 13.1 %collective-permute-start.12 = (bf16[768,256]{1,0:T(8,128)(2,1)S(1)}, bf16[768,256]{1,0:T(8,128)(2,1)S(1)}, u32[]{:S(2)}, u32[]{:S(2)}) collective-permute-start(bf16[768,256]{1,0:T(8,128)(2,1)S(1)} %convolution_convert_fusion.1), channel_id=1, source_target_pairs={{0,248},{4,252},{8,0},{12,4},{16,8},{20,12},{24,16},{28,20},{32,24... | collective-permute-start | bytes 1179656 | tf_op jit(solution)/shard_map/ppermute | solution.py:12
  224.8 15.7 %collective-permute-start.13 = (bf16[768,256]{1,0:T(8,128)(2,1)S(1)}, bf16[768,256]{1,0:T(8,128)(2,1)S(1)}, u32[]{:S(2)}, u32[]{:S(2)}) collective-permute-start(bf16[768,256]{1,0:T(8,128)(2,1)S(1)} %collective-permute-done.12), channel_id=1, source_target_pairs={{0,4},{4,8},{8,12},{12,16},{16,20},{20,24},{24,28},{28,32},{32,36}... | collective-permute-start | bytes 1179656 | tf_op jit(solution)/shard_map/ppermute | solution.py:12
  240.5 14.9 %collective-permute-start.14 = (bf16[768,256]{1,0:T(8,128)(2,1)S(1)}, bf16[768,256]{1,0:T(8,128)(2,1)S(1)}, u32[]{:S(2)}, u32[]{:S(2)}) collective-permute-start(bf16[768,256]{1,0:T(8,128)(2,1)S(1)} %collective-permute-done.13), channel_id=1, source_target_pairs={{0,4},{4,8},{8,12},{12,16},{16,20},{20,24},{24,28},{28,32},{32,36}... | collective-permute-start | bytes 1179656 | tf_op jit(solution)/shard_map/ppermute | solution.py:12
  255.4 14.0 %collective-permute-start.15 = (bf16[768,256]{1,0:T(8,128)(2,1)S(1)}, bf16[768,256]{1,0:T(8,128)(2,1)S(1)}, u32[]{:S(2)}, u32[]{:S(2)}) collective-permute-start(bf16[768,256]{1,0:T(8,128)(2,1)S(1)} %collective-permute-done.14), channel_id=1, source_target_pairs={{0,4},{4,8},{8,12},{12,16},{16,20},{20,24},{24,28},{28,32},{32,36}... | collective-permute-start | bytes 1179656 | tf_op jit(solution)/shard_map/ppermute | solution.py:12
  269.4 13.5 %collective-permute-start.16 = (bf16[768,256]{1,0:T(8,128)(2,1)S(1)}, bf16[768,256]{1,0:T(8,128)(2,1)S(1)}, u32[]{:S(2)}, u32[]{:S(2)}) collective-permute-start(bf16[768,256]{1,0:T(8,128)(2,1)S(1)} %collective-permute-done.15), channel_id=1, source_target_pairs={{0,4},{4,8},{8,12},{12,16},{16,20},{20,24},{24,28},{28,32},{32,36}... | collective-permute-start | bytes 1179656 | tf_op jit(solution)/shard_map/ppermute | solution.py:12
  297.0 13.6 %copy-start.3 = (f32[6,256,128,1]{1,2,3,0:T(8,128)}, f32[6,256,128,1]{1,2,3,0:T(8,128)S(1)}, u32[]{:S(2)}) copy-start(f32[6,256,128,1]{1,2,3,0:T(8,128)S(1)} %fusion.2) | copy-start | bytes 2359300
  297.1 9.7 %collective-permute-start.17 = (bf16[768,256]{1,0:T(8,128)(2,1)S(1)}, bf16[768,256]{1,0:T(8,128)(2,1)S(1)}, u32[]{:S(2)}, u32[]{:S(2)}) collective-permute-start(bf16[768,256]{1,0:T(8,128)(2,1)S(1)} %fusion.21), channel_id=1, source_target_pairs={{0,1},{2,3},{4,5},{6,7},{8,9},{10,11},{12,13},{14,15},{16,17},{18,... | collective-permute-start | bytes 1179656 | tf_op jit(solution)/shard_map/ppermute | solution.py:18
  310.6 13.1 %collective-permute-start.18 = (bf16[768,256]{1,0:T(8,128)(2,1)S(1)}, bf16[768,256]{1,0:T(8,128)(2,1)S(1)}, u32[]{:S(2)}, u32[]{:S(2)}) collective-permute-start(bf16[768,256]{1,0:T(8,128)(2,1)S(1)} %convolution_convert_fusion), channel_id=1, source_target_pairs={{0,248},{4,252},{8,0},{12,4},{16,8},{20,12},{24,16},{28,20},{32,24... | collective-permute-start | bytes 1179656 | tf_op jit(solution)/shard_map/ppermute | solution.py:12
  323.6 15.7 %collective-permute-start.19 = (bf16[768,256]{1,0:T(8,128)(2,1)S(1)}, bf16[768,256]{1,0:T(8,128)(2,1)S(1)}, u32[]{:S(2)}, u32[]{:S(2)}) collective-permute-start(bf16[768,256]{1,0:T(8,128)(2,1)S(1)} %collective-permute-done.18), channel_id=1, source_target_pairs={{0,4},{4,8},{8,12},{12,16},{16,20},{20,24},{24,28},{28,32},{32,36}... | collective-permute-start | bytes 1179656 | tf_op jit(solution)/shard_map/ppermute | solution.py:12
  339.3 14.9 %collective-permute-start.20 = (bf16[768,256]{1,0:T(8,128)(2,1)S(1)}, bf16[768,256]{1,0:T(8,128)(2,1)S(1)}, u32[]{:S(2)}, u32[]{:S(2)}) collective-permute-start(bf16[768,256]{1,0:T(8,128)(2,1)S(1)} %collective-permute-done.19), channel_id=1, source_target_pairs={{0,4},{4,8},{8,12},{12,16},{16,20},{20,24},{24,28},{28,32},{32,36}... | collective-permute-start | bytes 1179656 | tf_op jit(solution)/shard_map/ppermute | solution.py:12
  354.2 14.0 %collective-permute-start.21 = (bf16[768,256]{1,0:T(8,128)(2,1)S(1)}, bf16[768,256]{1,0:T(8,128)(2,1)S(1)}, u32[]{:S(2)}, u32[]{:S(2)}) collective-permute-start(bf16[768,256]{1,0:T(8,128)(2,1)S(1)} %collective-permute-done.20), channel_id=1, source_target_pairs={{0,4},{4,8},{8,12},{12,16},{16,20},{20,24},{24,28},{28,32},{32,36}... | collective-permute-start | bytes 1179656 | tf_op jit(solution)/shard_map/ppermute | solution.py:12
  368.2 13.5 %collective-permute-start.22 = (bf16[768,256]{1,0:T(8,128)(2,1)S(1)}, bf16[768,256]{1,0:T(8,128)(2,1)S(1)}, u32[]{:S(2)}, u32[]{:S(2)}) collective-permute-start(bf16[768,256]{1,0:T(8,128)(2,1)S(1)} %collective-permute-done.21), channel_id=1, source_target_pairs={{0,4},{4,8},{8,12},{12,16},{16,20},{20,24},{24,28},{28,32},{32,36}... | collective-permute-start | bytes 1179656 | tf_op jit(solution)/shard_map/ppermute | solution.py:12
  389.1 6.8 %copy-start.2 = (f32[6,256,128,1]{1,2,3,0:T(8,128)S(1)}, f32[6,256,128,1]{1,2,3,0:T(8,128)}, u32[]{:S(2)}) copy-start(f32[6,256,128,1]{1,2,3,0:T(8,128)} %copy-done.1) | copy-start | bytes 2359300
  389.1 6.8 %copy-start.4 = (f32[6,256,128,1]{1,2,3,0:T(8,128)S(1)}, f32[6,256,128,1]{1,2,3,0:T(8,128)}, u32[]{:S(2)}) copy-start(f32[6,256,128,1]{1,2,3,0:T(8,128)} %copy-done.3) | copy-start | bytes 2359300
where the time goes:
time: 398 us
  waiting for transfers between devices  306 us (77%)
  local copies, waits for them, and re-layouts  32.2 us (8%)
  matrix products  28.2 us (7%)
  starting transfers between devices  14.9 us (4%)
  blocking collectives  9.48 us (2%)
  other arithmetic  6.26 us (2%)
    ppermute x20, waiting for transfers between devices, shifted(): lax.ppermute(value, axis, [(i, (i + by) % devices) for i in range(devices)])  281 us
    gather x4, local copies, waits for them, and re-layouts, tile_products(): picked = blocks[columns]  29.1 us
    dot_general x4, matrix products, tile_products(): jnp.einsum('btij,btjf->bif', values, picked, preferred_element_type=jnp.f...  26.8 us
    ppermute x3, waiting for transfers between devices, shifted_2(): return lax.ppermute(value, axis, pairs)  25.1 us
    ppermute x20, starting transfers between devices, shifted(): lax.ppermute(value, axis, [(i, (i + by) % devices) for i in range(devices)])  11 us
    all_gather x4, blocking collectives, transform(): lax.all_gather(inputs, 'rep', axis=1, tiled=True)  9.48 us
  transfers between devices with their start and end apart: 23, of which 23 were waited for; matrix products, arithmetic and copies ran while one was open for 0% of the time, Pallas kernels for 0%

commit v1 on v0

v1 whole, which is shorter than its diff:
```python
import jax
import jax.numpy as jnp
from jax import lax
from jax.experimental import pallas as pl
from jax.experimental.pallas import tpu as pltpu
from jax.sharding import PartitionSpec as P

BLOCK = 128
REACH = 2
SLABS = 2 * REACH + 1
HIGH_Y = 2
NEAR = 4
MESH = pl.DeviceIdType.MESH
BF16 = jnp.bfloat16
F32 = jnp.float32


def mm(a, b):
    return jnp.dot(a, b, preferred_element_type=F32)


def kernel(
    slot_of,
    bias,
    features,
    weights,
    tile_vals,
    out,
    tiles,
    dense,
    own_s,
    own_m,
    win_s,
    win_m,
    acc_s,
    acc_m,
    ax_s,
    ax_m,
    hid_s,
    hid_m,
    w_first,
    w_second,
    b_first,
    b_second,
    out_s,
    out_m,
    local_sem,
    send_sem,
    win_sem,
    ax_sem,
    side_send,
    w_sem,
    out_sem,
):
    blk = lax.axis_index("blk")
    rep = lax.axis_index("rep")
    layer = lax.axis_index("layer")
    n_blk = lax.axis_size("blk")
    per_y = n_blk // HIGH_Y
    role = lax.rem(layer + blk // per_y, 2)
    main_snap = 2 * role
    nodes = own_s.shape[1]
    half = nodes // 2
    row_blocks = nodes // BLOCK

    def along(offset):
        other = lax.rem(blk + offset + n_blk, n_blk)
        return {"blk": other, "rep": rep, "layer": lax.rem(role + other // per_y, 2)}

    def here(flip_rep, flip_layer):
        return {
            "blk": blk,
            "rep": 1 - rep if flip_rep else rep,
            "layer": 1 - layer if flip_layer else layer,
        }

    def remote(src, dst, send, recv, device):
        return pltpu.make_async_remote_copy(
            src_ref=src, dst_ref=dst, send_sem=send, recv_sem=recv,
            device_id=device, device_id_type=MESH,
        )

    share = pl.ds(pl.multiple_of(role * BLOCK, BLOCK), BLOCK)
    load_s = pltpu.make_async_copy(features.at[1, :, share], own_s.at[0], local_sem.at[0])
    load_m = pltpu.make_async_copy(features.at[main_snap], own_m.at[0], local_sem.at[1])
    n_tiles = tile_vals.shape[0]
    load_t = pltpu.make_async_copy(tile_vals, tiles.at[pl.ds(0, n_tiles)], local_sem.at[2])
    load_w0 = pltpu.make_async_copy(weights.at[0], w_first.at[rep], local_sem.at[3])
    load_w1 = pltpu.make_async_copy(weights.at[0], w_second, local_sem.at[3])
    load_s.start()
    load_m.start()
    load_t.start()
    spread = jnp.broadcast_to(bias[...], (16, bias.shape[1]))

    @pl.when(layer == 0)
    def _():
        load_w0.start()
        b_first[rep] = spread

    @pl.when(layer == 1)
    def _():
        load_w1.start()
        b_second[...] = spread

    tiles[n_tiles] = jnp.zeros((BLOCK, BLOCK), BF16)

    barrier = pltpu.get_barrier_semaphore()
    partners = [along(o) for o in (1, -1, NEAR, -NEAR)]
    partners += [here(True, False), here(False, True), here(True, True)]
    for partner in partners:
        pl.semaphore_signal(barrier, inc=1, device_id=partner, device_id_type=MESH)
    pl.semaphore_wait(barrier, len(partners))

    sent = []

    class Exchange:
        def __init__(self, which):
            def window(slot, chunk):
                rows = pl.ds((chunk % 2) * half, half)
                return (win_s if chunk < 2 else win_m).at[which, slot, rows]

            def own(chunk):
                rows = pl.ds((chunk % 2) * half, half)
                return (own_s if chunk < 2 else own_m).at[which, rows]

            def copy(src, slot, chunk, offset):
                made = remote(
                    src, window(slot, chunk), send_sem.at[len(sent)],
                    win_sem.at[which, slot, chunk], along(offset),
                )
                sent.append(made)
                return made

            self.right = [copy(own(c), 1, c, 1) for c in range(4)]
            self.left = [copy(own(c), 2, c, -1) for c in range(4)]
            self.right2 = {c: copy(window(1, c), 0, c, 1) for c in (0, 2)}
            self.left2 = {c: copy(window(2, c), 3, c, -1) for c in (1, 3)}
            self.right4 = {c: copy(window(3, c), 0, c, NEAR) for c in (1, 3)}
            self.left4 = {c: copy(window(0, c), 3, c, -NEAR) for c in (0, 2)}

        def pass_on(self, base):
            self.right[base].wait_recv()
            self.right2[base].start()
            self.left[base + 1].wait_recv()
            self.left2[base + 1].start()

        def near_ready(self, base):
            self.right[base + 1].wait_recv()
            self.left[base].wait_recv()

        def pass_far(self, base):
            self.right2[base].wait_recv()
            self.left4[base].start()
            self.left2[base + 1].wait_recv()
            self.right4[base + 1].start()

        def far_ready(self, base):
            self.left4[base].wait_recv()
            self.right4[base + 1].wait_recv()

    first = Exchange(0)
    second = Exchange(1)

    load_s.wait()
    first.right[0].start()
    first.left[1].start()
    first.right[1].start()
    first.left[0].start()
    load_m.wait()
    first.right[2].start()
    first.left[3].start()

    def send_first(index, device):
        return (
            remote(w_first.at[rep], w_first.at[rep], side_send.at[2 * index], w_sem.at[rep], device),
            remote(b_first.at[rep], b_first.at[rep], side_send.at[2 * index + 1], w_sem.at[2 + rep], device),
        )

    to_core = send_first(0, here(True, False))
    to_layer = send_first(1, here(False, True))
    to_both = send_first(2, here(True, True))
    back = (
        remote(w_second, w_second, side_send.at[0], w_sem.at[4], here(False, True)),
        remote(b_second, b_second, side_send.at[1], w_sem.at[5], here(False, True)),
    )
    from_rep = [
        (
            remote(w_first.at[c], w_first.at[c], side_send.at[0], w_sem.at[c], here(True, False)),
            remote(b_first.at[c], b_first.at[c], side_send.at[0], w_sem.at[2 + c], here(True, False)),
        )
        for c in range(2)
    ]

    @pl.when(layer == 0)
    def _():
        load_w0.wait()
        for made in to_core + to_layer + to_both:
            made.start()

    @pl.when(layer == 1)
    def _():
        load_w1.wait()
        for made in back:
            made.start()

    load_t.wait()

    def lay_row(b, carry):
        rows = pl.ds(pl.multiple_of(b * BLOCK, BLOCK), BLOCK)
        for d in range(SLABS):
            for j in range(row_blocks):
                cols = pl.ds(j * BLOCK, BLOCK)
                dense[d, rows, cols] = tiles[slot_of[b, d * row_blocks + j]]
        return carry

    lax.fori_loop(0, row_blocks, lay_row, 0)

    def slab(which, main, d):
        if d == REACH:
            return (own_m if main else own_s)[which]
        slot = d if d < REACH else d - 1
        return (win_m if main else win_s)[which, slot]

    def gather(which, main, slabs, start):
        acc = acc_m if main else acc_s
        total = mm(dense[slabs[0]], slab(which, main, slabs[0]))
        for d in slabs[1:]:
            total = total + mm(dense[d], slab(which, main, d))
        if start:
            acc[...] = total
        else:
            acc[...] += total

    def side(index, src, dst, recv, device):
        return remote(src, dst, side_send.at[index], recv, device)

    quarter = 2 * rep + role
    first.pass_on(0)
    first.right[3].start()
    first.left[2].start()
    gather(0, False, (2,), True)
    first.near_ready(0)
    gather(0, False, (1, 3), False)
    first.pass_far(0)
    gather(0, True, (2,), True)
    first.pass_on(2)
    first.far_ready(0)
    gather(0, False, (0, 4), False)
    ax_s[quarter] = acc_s[...].astype(BF16)
    ax_sent = [
        side(6 + i, ax_s.at[quarter], ax_s.at[quarter], ax_sem.at[quarter], device)
        for i, device in enumerate((here(False, True), here(True, True), here(True, False)))
    ]
    for made in ax_sent:
        made.start()
    first.near_ready(2)
    gather(0, True, (1, 3), False)

    @pl.when(layer == 0)
    def _():
        other = 1 - rep
        remote(w_first.at[other], w_first.at[other], side_send.at[0], w_sem.at[other], here(True, False)).wait_recv()
        remote(b_first.at[other], b_first.at[other], side_send.at[0], w_sem.at[2 + other], here(True, False)).wait_recv()
        for made in back:
            made.wait_recv()

    @pl.when(layer == 1)
    def _():
        for pair in from_rep:
            for made in pair:
                made.wait_recv()

    def hidden(parts, target):
        width = parts[0].shape[1]
        for c in range(2):
            total = mm(parts[0], w_first[c, pl.ds(0, width)])
            for i in range(1, len(parts)):
                total = total + mm(parts[i], w_first[c, pl.ds(i * width, width)])
            total = total + b_first[c, pl.ds(0, 1)].astype(F32)
            target[c] = jnp.maximum(total, 0.0).astype(BF16)

    def wait_quarter(q):
        side(9, ax_s.at[q], ax_s.at[q], ax_sem.at[q], here(True, False)).wait_recv()

    wait_quarter(2 * rep + 1 - role)
    wait_quarter(2 * (1 - rep) + role)
    wait_quarter(2 * (1 - rep) + 1 - role)
    hidden([ax_s[q] for q in range(4)], hid_s)
    cols = w_second.shape[0] // 2
    own_s[1] = (
        mm(hid_s[0], w_second[pl.ds(0, cols), share]) + mm(hid_s[1], w_second[pl.ds(cols, cols), share])
    ).astype(BF16)
    second.right[0].start()
    second.left[1].start()
    second.right[1].start()
    second.left[0].start()
    first.pass_far(2)

    keep_s = pltpu.make_async_copy(hid_s.at[rep], out.at[1], local_sem.at[4])

    @pl.when(layer == 0)
    def _():
        keep_s.start()

    first.far_ready(2)
    gather(0, True, (0, 4), False)
    ax_m[rep] = acc_m[...].astype(BF16)
    ax_main = side(9, ax_m.at[rep], ax_m.at[rep], ax_sem.at[4 + rep], here(True, False))
    ax_main.start()
    second.pass_on(0)
    gather(1, False, (2,), True)
    side(10, ax_m.at[1 - rep], ax_m.at[1 - rep], ax_sem.at[5 - rep], here(True, False)).wait_recv()
    hidden([ax_m[0], ax_m[1]], hid_m)
    own_m[1] = (
        mm(hid_m[0], w_second[pl.ds(0, cols)]) + mm(hid_m[1], w_second[pl.ds(cols, cols)])
    ).astype(BF16)
    second.right[2].start()
    second.left[3].start()
    second.right[3].start()
    second.left[2].start()

    keep_m = pltpu.make_async_copy(hid_m.at[rep], out.at[main_snap], local_sem.at[5])
    give_m = side(10, hid_m.at[rep], out.at[main_snap], out_sem.at[0], here(False, True))

    @pl.when(layer == 0)
    def _():
        keep_m.start()

    @pl.when(layer == 1)
    def _():
        give_m.start()

    second.near_ready(0)
    gather(1, False, (1, 3), False)
    second.pass_far(0)
    gather(1, True, (2,), True)
    second.pass_on(2)
    second.far_ready(0)
    gather(1, False, (0, 4), False)
    row = b_second[pl.ds(0, 1)].astype(F32)
    row_s = b_second[pl.ds(0, 1), share].astype(F32)
    out_s[...] = (acc_s[...] + row_s).astype(BF16)
    put_s = pltpu.make_async_copy(out_s, out.at[1, :, share], local_sem.at[4])
    push_s = side(11, out_s, out.at[1, :, share], out_sem.at[1], here(False, True))

    @pl.when(layer == 1)
    def _():
        put_s.start()

    @pl.when(layer == 0)
    def _():
        push_s.start()

    second.near_ready(2)
    gather(1, True, (1, 3), False)
    second.pass_far(2)
    second.far_ready(2)
    gather(1, True, (0, 4), False)
    out_m[...] = (acc_m[...] + row).astype(BF16)
    put_m = pltpu.make_async_copy(out_m, out.at[main_snap], local_sem.at[5])
    push_m = side(12, out_m, out.at[main_snap], out_sem.at[2], here(False, True))

    @pl.when(layer == 1)
    def _():
        put_m.start()
        put_s.wait()
        put_m.wait()
        other_cols = pl.ds(pl.multiple_of((1 - role) * BLOCK, BLOCK), BLOCK)
        side(11, out_s, out.at[1, :, other_cols], out_sem.at[1], here(False, True)).wait_recv()
        side(12, out_m, out.at[2 - main_snap], out_sem.at[2], here(False, True)).wait_recv()
        give_m.wait_send()
        for made in back:
            made.wait_send()

    @pl.when(layer == 0)
    def _():
        push_m.start()
        keep_s.wait()
        keep_m.wait()
        side(10, hid_m.at[rep], out.at[2 - main_snap], out_sem.at[0], here(False, True)).wait_recv()
        push_s.wait_send()
        push_m.wait_send()
        for made in to_core + to_layer + to_both:
            made.wait_send()

    ax_main.wait_send()
    for made in ax_sent:
        made.wait_send()
    for made in sent:
        made.wait_send()


def per_device(features, weights, biases, tile_vals, tile_cols, tile_counts):
    row_blocks, slots = tile_cols.shape
    snaps, nodes, width = features.shape
    n_tiles = row_blocks * slots
    blk = lax.axis_index("blk")
    n_blk = lax.axis_size("blk")
    places = jnp.arange(SLABS * row_blocks, dtype=jnp.int32)
    targets = (places // row_blocks + blk - REACH + n_blk) % n_blk * row_blocks + places % row_blocks
    slot_ids = lax.broadcasted_iota(jnp.int32, tile_cols.shape, 1)
    flat_ids = lax.broadcasted_iota(jnp.int32, tile_cols.shape, 0) * slots + slot_ids
    found = (tile_cols[:, :, None] == targets) & (slot_ids < tile_counts[:, None])[:, :, None]
    slot_of = n_tiles + jnp.sum(jnp.where(found, flat_ids[:, :, None] - n_tiles, 0), axis=1)

    result = pl.pallas_call(
        kernel,
        out_shape=jax.ShapeDtypeStruct(features.shape, BF16),
        in_specs=[
            pl.BlockSpec(memory_space=pltpu.SMEM),
            pl.BlockSpec(memory_space=pltpu.VMEM),
            pl.BlockSpec(memory_space=pl.ANY),
            pl.BlockSpec(memory_space=pl.ANY),
            pl.BlockSpec(memory_space=pl.ANY),
        ],
        out_specs=pl.BlockSpec(memory_space=pl.ANY),
        scratch_shapes=[
            pltpu.VMEM((n_tiles + 1, BLOCK, BLOCK), BF16),
            pltpu.VMEM((SLABS, nodes, nodes), BF16),
            pltpu.VMEM((2, nodes, BLOCK), BF16),
            pltpu.VMEM((2, nodes, width), BF16),
            pltpu.VMEM((2, 2 * REACH, nodes, BLOCK), BF16),
            pltpu.VMEM((2, 2 * REACH, nodes, width), BF16),
            pltpu.VMEM((nodes, BLOCK), F32),
            pltpu.VMEM((nodes, width), F32),
            pltpu.VMEM((4, nodes, BLOCK), BF16),
            pltpu.VMEM((2, nodes, width), BF16),
            pltpu.VMEM((2, nodes, width), BF16),
            pltpu.VMEM((2, nodes, width), BF16),
            pltpu.VMEM((2, 2 * width, width), BF16),
            pltpu.VMEM((2 * width, width), BF16),
            pltpu.VMEM((2, 16, width), BF16),
            pltpu.VMEM((16, width), BF16),
            pltpu.VMEM((nodes, BLOCK), BF16),
            pltpu.VMEM((nodes, width), BF16),
            pltpu.SemaphoreType.DMA((6,)),
            pltpu.SemaphoreType.DMA((32,)),
            pltpu.SemaphoreType.DMA((2, 2 * REACH, 4)),
            pltpu.SemaphoreType.DMA((6,)),
            pltpu.SemaphoreType.DMA((13,)),
            pltpu.SemaphoreType.DMA((6,)),
            pltpu.SemaphoreType.DMA((3,)),
        ],
        compiler_params=pltpu.CompilerParams(
            collective_id=0, has_side_effects=True, vmem_limit_bytes=48 * 1024 * 1024
        ),
    )(slot_of, biases, features, weights, tile_vals.reshape(n_tiles, BLOCK, BLOCK))
    return result[None]


def solution(mesh):
    return jax.shard_map(
        per_device,
        mesh=mesh,
        in_specs=(
            P(None, "blk", "rep"),
            P("layer", None, "rep"),
            P("layer", "rep"),
            P("blk", None, None, None),
            P("blk", None),
            P("blk"),
        ),
        out_specs=P("layer", None, "blk", "rep"),
        check_vma=False,
    )
```

time: 398 us -> 97.1 us (0.24)
  the two profiles are of different devices: /device:TPU:8 before, /device:TPU:14 now
where the time goes in v1:
time: 97.1 us; the launch traced here: 96.9 us
  Pallas kernels  91.3 us (94%)
  local copies, waits for them, and re-layouts  3.91 us (4%)
  other arithmetic  1.64 us (2%)
    pallas_call x1, Pallas kernels, per_device(): pl.pallas_call(kernel, out_shape=jax.ShapeDtypeStruct(features.shape, BF1...  91.3 us
    unnamed x7, local copies, waits for them, and re-layouts  3.91 us

profile of v1, /device:TPU:14, one launch (start us, length us, event | category | flops | bytes accessed | tf_op | source)
XLA Modules:
  0.0 96.9 jit_solution(12080884510956928589)
XLA Ops:
  0.0 0.7 iota_compare_fusion
  0.8 0.1 add_add_fusion
  0.8 0.8 select_reduce_fusion
  1.7 0.0 copy-start
  1.7 1.3 %copy-done = bf16[3,768,256]{2,1,0:T(8,128)(2,1)S(1)} copy-done((bf16[3,768,256]{2,1,0:T(8,128)(2,1)S(1)}, bf16[3,768,256]{2,1,0:T(8,128)(2,1)}, u32[]{:S(2)}) %copy-start) | copy-done | bytes 1179672
  2.9 0.0 copy-start.1
  2.9 0.9 copy-done.1
  3.9 0.0 copy-start.2
  3.9 0.7 copy-done.2
  4.6 91.3 %shard_map.64 = bf16[3,768,256]{2,1,0:T(8,128)(2,1)S(1)} custom-call(s32[6,30]{1,0:T(8,128)S(1)} %broadcast_add_fusion.slot_of, bf16[1,256]{1,0:T(2,128)(2,1)S(1)} %copy-done.2, bf16[3,768,256]{2,1,0:T(8,128)(2,1)S(1)} %copy-done, bf16[1,512,256]{2,1,0:T(8,128)(2,1)S(1)} %copy-done.1, bf16[144,128,128]{2,1,0:T(8,128)(2,1)} %bitcast.3), custom_call_target="tpu_custom_call" | custom-call | tf_op jit(solution)/shard_map/pallas_call | solution.py:406
  95.8 1.0 %copy.8 = bf16[1,3,768,256]{3,2,1,0:T(8,128)(2,1)} copy(bf16[1,3,768,256]{3,2,1,0:T(8,128)(2,1)S(1)} %bitcast.2) | data formatting | bytes 2359296
  (3 shorter events, 0.0 us)
Async XLA Ops:
  1.7 1.3 %copy-start = (bf16[3,768,256]{2,1,0:T(8,128)(2,1)S(1)}, bf16[3,768,256]{2,1,0:T(8,128)(2,1)}, u32[]{:S(2)}) copy-start(bf16[3,768,256]{2,1,0:T(8,128)(2,1)} %features.1) | copy-start | bytes 3538948
  2.9 0.9 copy-start.1
  3.9 0.7 copy-start.2

commit v2 on v1

v2 whole, which is shorter than its diff:
```python
import jax
import jax.numpy as jnp
from jax import lax
from jax.experimental import pallas as pl
from jax.experimental.pallas import tpu as pltpu
from jax.sharding import PartitionSpec as P

BLOCK = 128
REACH = 2
SLABS = 2 * REACH + 1
HIGH_Y = 2
CHUNKS = 6
MESH = pl.DeviceIdType.MESH
BF16 = jnp.bfloat16
F32 = jnp.float32


def mm(a, b):
    return jnp.dot(a, b, preferred_element_type=F32)


def kernel(
    counts,
    bias,
    tile_cols,
    features,
    weights,
    tile_vals,
    out,
    table,
    slot_of,
    tiles,
    dense,
    own_s,
    own_m,
    own_p,
    win_s,
    win_m,
    win_p,
    acc_s,
    acc_m,
    ax_s,
    ax_m,
    hid_s,
    hid_m,
    w_first,
    w_second,
    b_first,
    b_second,
    out_p,
    local_sem,
    send_sem,
    win_sem,
    ax_sem,
    side_send,
    w_sem,
    out_sem,
):
    blk = lax.axis_index("blk")
    rep = lax.axis_index("rep")
    layer = lax.axis_index("layer")
    n_blk = lax.axis_size("blk")
    per_y = n_blk // HIGH_Y
    role = lax.rem(layer + blk // per_y, 2)
    main_snap = 2 * role
    nodes = own_s.shape[0]
    row_blocks = nodes // BLOCK
    n_tiles = tile_vals.shape[0]
    slots = n_tiles // row_blocks

    def along(offset):
        other = lax.rem(blk + offset + n_blk, n_blk)
        return {"blk": other, "rep": rep, "layer": lax.rem(role + other // per_y, 2)}

    def here(flip_rep, flip_layer):
        return {
            "blk": blk,
            "rep": 1 - rep if flip_rep else rep,
            "layer": 1 - layer if flip_layer else layer,
        }

    to_core, to_layer = here(True, False), here(False, True)

    def remote(src, dst, send, recv, device):
        return pltpu.make_async_remote_copy(
            src_ref=src, dst_ref=dst, send_sem=send, recv_sem=recv,
            device_id=device, device_id_type=MESH,
        )

    barrier = pltpu.get_barrier_semaphore()
    partners = [along(1), along(-1), to_core, to_layer]
    for partner in partners:
        pl.semaphore_signal(barrier, inc=1, device_id=partner, device_id_type=MESH)

    share = pl.ds(pl.multiple_of(role * BLOCK, BLOCK), BLOCK)
    load_s = pltpu.make_async_copy(features.at[1, :, share], own_s, local_sem.at[0])
    load_m = pltpu.make_async_copy(features.at[main_snap], own_m, local_sem.at[1])
    load_t = pltpu.make_async_copy(tile_vals, tiles.at[pl.ds(0, n_tiles)], local_sem.at[2])
    load_w0 = pltpu.make_async_copy(weights.at[0], w_first.at[rep], local_sem.at[3])
    load_w1 = pltpu.make_async_copy(weights.at[0], w_second, local_sem.at[3])
    load_s.start()
    load_m.start()
    load_t.start()
    spread = jnp.broadcast_to(bias[...], (16, bias.shape[1]))

    @pl.when(layer == 0)
    def _():
        load_w0.start()
        b_first[rep] = spread

    @pl.when(layer == 1)
    def _():
        load_w1.start()
        b_second[...] = spread

    tiles[n_tiles] = jnp.zeros((BLOCK, BLOCK), BF16)

    row_ids = lax.broadcasted_iota(jnp.int32, (row_blocks, slots), 0)
    slot_ids = lax.broadcasted_iota(jnp.int32, (row_blocks, slots), 1)
    live = jnp.zeros((row_blocks, slots), jnp.int32)
    for b in range(row_blocks):
        live = jnp.where(row_ids == b, counts[b], live)
    columns = jnp.where(slot_ids < live, tile_cols[...], -1)
    flat_ids = row_ids * slots + slot_ids - n_tiles
    lanes = lax.broadcasted_iota(jnp.int32, (row_blocks, BLOCK), 1)
    found = jnp.full((row_blocks, BLOCK), n_tiles, jnp.int32)
    for d in range(SLABS):
        first_block = lax.rem(blk + d - REACH + n_blk, n_blk) * row_blocks
        for j in range(row_blocks):
            hit = jnp.where(columns == first_block + j, flat_ids, 0)
            at = jnp.sum(hit, axis=1, keepdims=True)
            found = jnp.where(lanes == d * row_blocks + j, found + at, found)
    table[pl.ds(0, row_blocks)] = found

    pl.semaphore_wait(barrier, len(partners))

    sent = []

    class Exchange:
        def __init__(self, which, own, window):
            def copy(src, slot, chunk, offset):
                made = remote(
                    src, window(slot, chunk), send_sem.at[len(sent)],
                    win_sem.at[which, slot, chunk], along(offset),
                )
                sent.append(made)
                return made

            every = range(CHUNKS)
            self.right = [copy(own(c), 1, c, 1) for c in every]
            self.left = [copy(own(c), 2, c, -1) for c in every]
            self.right2 = [copy(window(1, c), 0, c, 1) for c in every]
            self.left2 = [copy(window(2, c), 3, c, -1) for c in every]

        def send(self, *chunks):
            for c in chunks:
                self.right[c].start()
                self.left[c].start()

        def pass_on(self, *chunks):
            for c in chunks:
                self.right[c].wait_recv()
                self.right2[c].start()
                self.left[c].wait_recv()
                self.left2[c].start()

        def far_ready(self, *chunks):
            for c in chunks:
                self.right2[c].wait_recv()
                self.left2[c].wait_recv()

    def half_rows(c):
        return pl.ds((c % 2) * (nodes // 2), nodes // 2)

    def main_rows(c):
        return pl.ds((c - 2) * (nodes // 4), nodes // 4)

    first = Exchange(
        0,
        lambda c: own_s.at[half_rows(c)] if c < 2 else own_m.at[main_rows(c)],
        lambda slot, c: win_s.at[slot, half_rows(c)] if c < 2 else win_m.at[slot, main_rows(c)],
    )
    second = Exchange(
        1,
        lambda c: own_p.at[c // 2, half_rows(c)],
        lambda slot, c: win_p.at[c // 2, slot, half_rows(c)],
    )

    load_s.wait()
    first.send(0, 1)
    load_m.wait()
    first.send(2)
    load_table = pltpu.make_async_copy(table, slot_of, local_sem.at[6])
    load_table.start()

    def side(index, src, dst, recv, device):
        return remote(src, dst, side_send.at[index], recv, device)

    def first_layer(index, c, device):
        return (
            side(index, w_first.at[c], w_first.at[c], w_sem.at[c], device),
            side(index + 1, b_first.at[c], b_first.at[c], w_sem.at[2 + c], device),
        )

    first_to_layer = first_layer(0, rep, to_layer)
    first_to_core = first_layer(2, rep, to_core)
    first_other = first_layer(2, 1 - rep, to_core)
    second_back = (
        side(0, w_second, w_second, w_sem.at[4], to_layer),
        side(1, b_second, b_second, w_sem.at[5], to_layer),
    )

    @pl.when(layer == 0)
    def _():
        load_w0.wait()
        for made in first_to_layer + first_to_core:
            made.start()

    @pl.when(layer == 1)
    def _():
        load_w1.wait()
        for made in second_back:
            made.start()

    load_table.wait()
    load_t.wait()

    def lay_row(b, carry):
        rows = pl.ds(pl.multiple_of(b * BLOCK, BLOCK), BLOCK)
        for d in range(SLABS):
            for j in range(row_blocks):
                cols = pl.ds(j * BLOCK, BLOCK)
                dense[d, rows, cols] = tiles[slot_of[b, d * row_blocks + j]]
        return carry

    lax.fori_loop(0, row_blocks, lay_row, 0)

    def gather(acc, slab, slabs, start):
        total = mm(dense[slabs[0]], slab(slabs[0]))
        for d in slabs[1:]:
            total = total + mm(dense[d], slab(d))
        if start:
            acc[...] = total
        else:
            acc[...] += total

    def part(own, win):
        return lambda d: own[...] if d == REACH else win[d if d < REACH else d - 1]

    part_s, part_m = part(own_s, win_s), part(own_m, win_m)
    parts = [part(own_p.at[p], win_p.at[p]) for p in range(3)]

    first.pass_on(0, 1)
    first.send(3, 4)
    gather(acc_s, part_s, (1, 2, 3), True)
    first.pass_on(2)
    first.send(5)
    first.far_ready(0, 1)
    gather(acc_s, part_s, (0, 4), False)
    quarter = 2 * rep + role
    ax_s[quarter] = acc_s[...].astype(BF16)
    across = side(4, ax_s.at[quarter], ax_s.at[quarter], ax_sem.at[quarter], to_layer)
    beside = side(5, ax_s.at[quarter], ax_s.at[quarter], ax_sem.at[quarter], to_core)
    across.start()
    beside.start()
    first.pass_on(3)

    @pl.when(layer == 1)
    def _():
        for made in first_layer(0, rep, to_layer):
            made.wait_recv()
        for made in first_to_core:
            made.start()

    gather(acc_m, part_m, (2,), True)
    first.pass_on(4)
    theirs = 2 * rep + 1 - role
    relayed = side(6, ax_s.at[theirs], ax_s.at[theirs], ax_sem.at[theirs], to_core)
    first.pass_on(5)
    relayed.wait_recv()
    relayed.start()
    gather(acc_m, part_m, (1, 3), False)
    for made in first_other:
        made.wait_recv()

    @pl.when(layer == 0)
    def _():
        for made in second_back:
            made.wait_recv()

    def hidden(pieces, target):
        width = pieces[0].shape[1]
        for c in range(2):
            total = mm(pieces[0], w_first[c, pl.ds(0, width)])
            for i in range(1, len(pieces)):
                total = total + mm(pieces[i], w_first[c, pl.ds(i * width, width)])
            total = total + b_first[c, pl.ds(0, 1)].astype(F32)
            target[c] = jnp.maximum(total, 0.0).astype(BF16)

    for q in (2 * (1 - rep) + role, 2 * (1 - rep) + 1 - role):
        side(6, ax_s.at[q], ax_s.at[q], ax_sem.at[q], to_core).wait_recv()
    hidden([ax_s[q] for q in range(4)], hid_s)
    cols = w_second.shape[0] // 2
    own_p[0] = (
        mm(hid_s[0], w_second[pl.ds(0, cols), share]) + mm(hid_s[1], w_second[pl.ds(cols, cols), share])
    ).astype(BF16)
    second.send(0, 1)
    first.far_ready(2, 3, 4, 5)
    gather(acc_m, part_m, (0, 4), False)
    ax_m[rep] = acc_m[...].astype(BF16)
    ax_main = side(7, ax_m.at[rep], ax_m.at[rep], ax_sem.at[4 + rep], to_core)
    ax_main.start()
    second.pass_on(0, 1)

    keep_s = pltpu.make_async_copy(hid_s.at[rep], out.at[1], local_sem.at[4])

    @pl.when(layer == 0)
    def _():
        keep_s.start()

    side(7, ax_m.at[1 - rep], ax_m.at[1 - rep], ax_sem.at[5 - rep], to_core).wait_recv()
    hidden([ax_m[0], ax_m[1]], hid_m)
    second_m = mm(hid_m[0], w_second[pl.ds(0, cols)]) + mm(hid_m[1], w_second[pl.ds(cols, cols)])
    own_p[1] = second_m[:, :BLOCK].astype(BF16)
    own_p[2] = second_m[:, BLOCK:].astype(BF16)
    second.send(2, 3, 4)

    keep_m = pltpu.make_async_copy(hid_m.at[rep], out.at[main_snap], local_sem.at[5])
    give_m = side(8, hid_m.at[rep], out.at[main_snap], out_sem.at[3], to_layer)

    @pl.when(layer == 0)
    def _():
        keep_m.start()

    @pl.when(layer == 1)
    def _():
        give_m.start()

    def piece_at(p, their_role):
        if p == 0:
            return out.at[1, :, pl.ds(pl.multiple_of(their_role * BLOCK, BLOCK), BLOCK)]
        return out.at[2 * their_role, :, pl.ds((p - 1) * BLOCK, BLOCK)]

    put = [pltpu.make_async_copy(out_p.at[p], piece_at(p, role), local_sem.at[7 + p]) for p in range(3)]
    push = [side(9 + p, out_p.at[p], piece_at(p, role), out_sem.at[p], to_layer) for p in range(3)]
    take = [side(9 + p, out_p.at[p], piece_at(p, 1 - role), out_sem.at[p], to_layer) for p in range(3)]

    def finish(p):
        gather(acc_s, parts[p], (0, 4), False)
        if p == 0:
            row = b_second[pl.ds(0, 1), share]
        else:
            row = b_second[pl.ds(0, 1), pl.ds((p - 1) * BLOCK, BLOCK)]
        out_p[p] = (acc_s[...] + row.astype(F32)).astype(BF16)

        @pl.when(layer == 1)
        def _():
            put[p].start()

        @pl.when(layer == 0)
        def _():
            push[p].start()

    gather(acc_s, parts[0], (1, 2, 3), True)
    second.far_ready(0, 1)
    finish(0)
    second.pass_on(2, 3)
    second.send(5)
    gather(acc_s, parts[1], (1, 2, 3), True)
    second.pass_on(4)
    second.far_ready(2, 3)
    finish(1)
    second.pass_on(5)
    gather(acc_s, parts[2], (1, 2, 3), True)
    second.far_ready(4, 5)
    finish(2)

    @pl.when(layer == 1)
    def _():
        for made in put:
            made.wait()
        for made in take:
            made.wait_recv()
        give_m.wait_send()
        for made in second_back + first_to_core:
            made.wait_send()

    @pl.when(layer == 0)
    def _():
        keep_s.wait()
        keep_m.wait()
        side(8, hid_m.at[rep], out.at[2 - main_snap], out_sem.at[3], to_layer).wait_recv()
        for made in push:
            made.wait_send()
        for made in first_to_layer + first_to_core:
            made.wait_send()

    for made in [ax_main, across, beside, relayed] + sent:
        made.wait_send()


def per_device(features, weights, biases, tile_vals, tile_cols, tile_counts):
    row_blocks, slots = tile_cols.shape
    snaps, nodes, width = features.shape
    n_tiles = row_blocks * slots
    tile_vals = tile_vals.reshape(n_tiles, BLOCK, BLOCK)
    features, weights, biases, tile_vals, tile_cols, tile_counts = (
        pltpu.with_memory_space_constraint(a, pltpu.HBM)
        for a in (features, weights, biases, tile_vals, tile_cols, tile_counts)
    )
    result = pl.pallas_call(
        kernel,
        out_shape=jax.ShapeDtypeStruct(features.shape, BF16),
        in_specs=[
            pl.BlockSpec(memory_space=pltpu.SMEM),
            pl.BlockSpec(memory_space=pltpu.VMEM),
            pl.BlockSpec(memory_space=pltpu.VMEM),
            pl.BlockSpec(memory_space=pl.ANY),
            pl.BlockSpec(memory_space=pl.ANY),
            pl.BlockSpec(memory_space=pl.ANY),
        ],
        out_specs=pl.BlockSpec(memory_space=pl.ANY),
        scratch_shapes=[
            pltpu.VMEM((8, BLOCK), jnp.int32),
            pltpu.SMEM((8, BLOCK), jnp.int32),
            pltpu.VMEM((n_tiles + 1, BLOCK, BLOCK), BF16),
            pltpu.VMEM((SLABS, nodes, nodes), BF16),
            pltpu.VMEM((nodes, BLOCK), BF16),
            pltpu.VMEM((nodes, width), BF16),
            pltpu.VMEM((3, nodes, BLOCK), BF16),
            pltpu.VMEM((2 * REACH, nodes, BLOCK), BF16),
            pltpu.VMEM((2 * REACH, nodes, width), BF16),
            pltpu.VMEM((3, 2 * REACH, nodes, BLOCK), BF16),
            pltpu.VMEM((nodes, BLOCK), F32),
            pltpu.VMEM((nodes, width), F32),
            pltpu.VMEM((4, nodes, BLOCK), BF16),
            pltpu.VMEM((2, nodes, width), BF16),
            pltpu.VMEM((2, nodes, width), BF16),
            pltpu.VMEM((2, nodes, width), BF16),
            pltpu.VMEM((2, 2 * width, width), BF16),
            pltpu.VMEM((2 * width, width), BF16),
            pltpu.VMEM((2, 16, width), BF16),
            pltpu.VMEM((16, width), BF16),
            pltpu.VMEM((3, nodes, BLOCK), BF16),
            pltpu.SemaphoreType.DMA((10,)),
            pltpu.SemaphoreType.DMA((8 * CHUNKS,)),
            pltpu.SemaphoreType.DMA((2, 2 * REACH, CHUNKS)),
            pltpu.SemaphoreType.DMA((6,)),
            pltpu.SemaphoreType.DMA((12,)),
            pltpu.SemaphoreType.DMA((6,)),
            pltpu.SemaphoreType.DMA((4,)),
        ],
        compiler_params=pltpu.CompilerParams(
            collective_id=0, has_side_effects=True, vmem_limit_bytes=48 * 1024 * 1024
        ),
    )(tile_counts, biases, tile_cols, features, weights, tile_vals)
    return result[None]


def solution(mesh):
    return jax.shard_map(
        per_device,
        mesh=mesh,
        in_specs=(
            P(None, "blk", "rep"),
            P("layer", None, "rep"),
            P("layer", "rep"),
            P("blk", None, None, None),
            P("blk", None),
            P("blk"),
        ),
        out_specs=P("layer", None, "blk", "rep"),
        check_vma=False,
    )
```

time: 97.1 us -> 80.7 us (0.83)
  the two profiles are of different devices: /device:TPU:14 before, /device:TPU:8 now
where the time goes in v2:
time: 80.7 us; the launch traced here: 80.6 us
  Pallas kernels  79.6 us (99%)
  local copies, waits for them, and re-layouts  1.02 us (1%)
    pallas_call x1, Pallas kernels, per_device(): pl.pallas_call(kernel, out_shape=jax.ShapeDtypeStruct(features.shape, BF1...  79.6 us

profile of v2, /device:TPU:8, one launch (start us, length us, event | category | flops | bytes accessed | tf_op | source)
XLA Modules:
  0.0 80.6 jit_solution(5804316213599272188)
XLA Ops:
  0.0 79.6 %shard_map.64 = bf16[3,768,256]{2,1,0:T(8,128)(2,1)S(1)} custom-call(s32[6]{0:T(128)} %counts.1, bf16[1,256]{1,0:T(2,128)(2,1)} %bias.1, s32[6,24]{1,0:T(8,128)} %tile_cols.1, bf16[3,768,256]{2,1,0:T(8,128)(2,1)} %features.1, bf16[1,512,256]{2,1,0:T(8,128)(2,1)} %weights.1, bf16[144,128,128]{2,1,0:T(8,128)(2,1)} %bitcast.3), custom_call_target="tpu_custom_call" | custom-call | tf_op jit(solution)/shard_map/pallas_call | solution.py:411
  79.6 1.0 %copy.8 = bf16[1,3,768,256]{3,2,1,0:T(8,128)(2,1)} copy(bf16[1,3,768,256]{3,2,1,0:T(8,128)(2,1)S(1)} %bitcast.2) | data formatting | bytes 2359296

commit v3 on v2

--- a/solution.py
+++ b/solution.py
@@ -9,7 +9,8 @@
 REACH = 2
 SLABS = 2 * REACH + 1
 HIGH_Y = 2
-CHUNKS = 6
+CUTS = ((0, 512), (512, 256))
+MAIN_ROWS = 256
 MESH = pl.DeviceIdType.MESH
 BF16 = jnp.bfloat16
 F32 = jnp.float32
@@ -137,7 +138,7 @@
     sent = []
 
     class Exchange:
-        def __init__(self, which, own, window):
+        def __init__(self, which, chunks, own, window):
             def copy(src, slot, chunk, offset):
                 made = remote(
                     src, window(slot, chunk), send_sem.at[len(sent)],
@@ -146,7 +147,7 @@
                 sent.append(made)
                 return made
 
-            every = range(CHUNKS)
+            every = range(chunks)
             self.right = [copy(own(c), 1, c, 1) for c in every]
             self.left = [copy(own(c), 2, c, -1) for c in every]
             self.right2 = [copy(window(1, c), 0, c, 1) for c in every]
@@ -169,21 +170,24 @@
                 self.right2[c].wait_recv()
                 self.left2[c].wait_recv()
 
-    def half_rows(c):
-        return pl.ds((c % 2) * (nodes // 2), nodes // 2)
+    def cut_rows(c):
+        return pl.ds(*CUTS[c % 2])
 
     def main_rows(c):
-        return pl.ds((c - 2) * (nodes // 4), nodes // 4)
-
+        return pl.ds((c - 2) * MAIN_ROWS, MAIN_ROWS)
+
+    main_chunks = nodes // MAIN_ROWS
     first = Exchange(
         0,
-        lambda c: own_s.at[half_rows(c)] if c < 2 else own_m.at[main_rows(c)],
-        lambda slot, c: win_s.at[slot, half_rows(c)] if c < 2 else win_m.at[slot, main_rows(c)],
+        2 + main_chunks,
+        lambda c: own_s.at[cut_rows(c)] if c < 2 else own_m.at[main_rows(c)],
+        lambda slot, c: win_s.at[slot, cut_rows(c)] if c < 2 else win_m.at[slot, main_rows(c)],
     )
     second = Exchange(
         1,
-        lambda c: own_p.at[c // 2, half_rows(c)],
-        lambda slot, c: win_p.at[c // 2, slot, half_rows(c)],
+        6,
+        lambda c: own_p.at[c // 2, cut_rows(c)],
+        lambda slot, c: win_p.at[c // 2, slot, cut_rows(c)],
     )
 
     load_s.wait()
@@ -235,28 +239,27 @@
 
     lax.fori_loop(0, row_blocks, lay_row, 0)
 
-    def gather(acc, slab, slabs, start):
-        total = mm(dense[slabs[0]], slab(slabs[0]))
-        for d in slabs[1:]:
-            total = total + mm(dense[d], slab(d))
+    everything = pl.ds(0, nodes)
+
+    def gather(acc, own, win, slabs, start=False, depth=everything, rows=everything):
+        total = None
+        for d in slabs:
+            slab = own[depth] if d == REACH else win[d if d < REACH else d - 1, depth]
+            product = mm(dense[d, rows, depth], slab)
+            total = product if total is None else total + product
         if start:
-            acc[...] = total
+            acc[rows] = total
         else:
-            acc[...] += total
-
-    def part(own, win):
-        return lambda d: own[...] if d == REACH else win[d if d < REACH else d - 1]
-
-    part_s, part_m = part(own_s, win_s), part(own_m, win_m)
-    parts = [part(own_p.at[p], win_p.at[p]) for p in range(3)]
-
+            acc[rows] += total
+
+    near, far = (1, 3), (0, 4)
     first.pass_on(0, 1)
-    first.send(3, 4)
-    gather(acc_s, part_s, (1, 2, 3), True)
+    first.send(3)
+    gather(acc_s, own_s, win_s, (2,) + near, True)
     first.pass_on(2)
-    first.send(5)
+    first.send(4)
     first.far_ready(0, 1)
-    gather(acc_s, part_s, (0, 4), False)
+    gather(acc_s, own_s, win_s, far)
     quarter = 2 * rep + role
     ax_s[quarter] = acc_s[...].astype(BF16)
     across = side(4, ax_s.at[quarter], ax_s.at[quarter], ax_sem.at[quarter], to_layer)
@@ -267,19 +270,17 @@
 
     @pl.when(layer == 1)
     def _():
-        for made in first_layer(0, rep, to_layer):
+        for made in first_to_layer:
             made.wait_recv()
         for made in first_to_core:
             made.start()
 
-    gather(acc_m, part_m, (2,), True)
-    first.pass_on(4)
+    gather(acc_m, own_m, win_m, (2,), True)
     theirs = 2 * rep + 1 - role
     relayed = side(6, ax_s.at[theirs], ax_s.at[theirs], ax_sem.at[theirs], to_core)
-    first.pass_on(5)
     relayed.wait_recv()
     relayed.start()
-    gather(acc_m, part_m, (1, 3), False)
+    first.pass_on(4)
     for made in first_other:
         made.wait_recv()
 
@@ -288,29 +289,41 @@
         for made in second_back:
             made.wait_recv()
 
-    def hidden(pieces, target):
+    def hidden(pieces, target, rows):
         width = pieces[0].shape[1]
         for c in range(2):
-            total = mm(pieces[0], w_first[c, pl.ds(0, width)])
+            total = mm(pieces[0][rows], w_first[c, pl.ds(0, width)])
             for i in range(1, len(pieces)):
-                total = total + mm(pieces[i], w_first[c, pl.ds(i * width, width)])
+                total = total + mm(pieces[i][rows], w_first[c, pl.ds(i * width, width)])
             total = total + b_first[c, pl.ds(0, 1)].astype(F32)
-            target[c] = jnp.maximum(total, 0.0).astype(BF16)
-
+            target[c, rows] = jnp.maximum(total, 0.0).astype(BF16)
+
+    cols = w_second.shape[0] // 2
+    quarters = [ax_s.at[q] for q in range(4)]
     for q in (2 * (1 - rep) + role, 2 * (1 - rep) + 1 - role):
         side(6, ax_s.at[q], ax_s.at[q], ax_sem.at[q], to_core).wait_recv()
-    hidden([ax_s[q] for q in range(4)], hid_s)
-    cols = w_second.shape[0] // 2
-    own_p[0] = (
-        mm(hid_s[0], w_second[pl.ds(0, cols), share]) + mm(hid_s[1], w_second[pl.ds(cols, cols), share])
-    ).astype(BF16)
-    second.send(0, 1)
-    first.far_ready(2, 3, 4, 5)
-    gather(acc_m, part_m, (0, 4), False)
-    ax_m[rep] = acc_m[...].astype(BF16)
-    ax_main = side(7, ax_m.at[rep], ax_m.at[rep], ax_sem.at[4 + rep], to_core)
-    ax_main.start()
-    second.pass_on(0, 1)
+    for c in range(2):
+        rows = cut_rows(c)
+        hidden(quarters, hid_s, rows)
+        own_p[0, rows] = (
+            mm(hid_s[0, rows], w_second[pl.ds(0, cols), share])
+            + mm(hid_s[1, rows], w_second[pl.ds(cols, cols), share])
+        ).astype(BF16)
+        second.send(c)
+
+    gather(acc_m, own_m, win_m, near)
+    for c in range(2, 1 + main_chunks):
+        first.far_ready(c)
+        gather(acc_m, own_m, win_m, far, depth=main_rows(c))
+    first.far_ready(1 + main_chunks)
+    ax_main = []
+    for c in range(2):
+        rows = cut_rows(c)
+        gather(acc_m, own_m, win_m, far, depth=main_rows(1 + main_chunks), rows=rows)
+        ax_m[rep, rows] = acc_m[rows].astype(BF16)
+        mine = ax_m.at[rep, rows]
+        ax_main.append(side(7 + c, mine, mine, ax_sem.at[4 + 2 * rep + c], to_core))
+        ax_main[c].start()
 
     keep_s = pltpu.make_async_copy(hid_s.at[rep], out.at[1], local_sem.at[4])
 
@@ -318,15 +331,22 @@
     def _():
         keep_s.start()
 
-    side(7, ax_m.at[1 - rep], ax_m.at[1 - rep], ax_sem.at[5 - rep], to_core).wait_recv()
-    hidden([ax_m[0], ax_m[1]], hid_m)
-    second_m = mm(hid_m[0], w_second[pl.ds(0, cols)]) + mm(hid_m[1], w_second[pl.ds(cols, cols)])
-    own_p[1] = second_m[:, :BLOCK].astype(BF16)
-    own_p[2] = second_m[:, BLOCK:].astype(BF16)
-    second.send(2, 3, 4)
+    for c in range(2):
+        second.pass_on(c)
+        rows = cut_rows(c)
+        other = ax_m.at[1 - rep, rows]
+        side(7 + c, other, other, ax_sem.at[6 - 2 * rep + c], to_core).wait_recv()
+        hidden([ax_m.at[0], ax_m.at[1]], hid_m, rows)
+        second_m = (
+            mm(hid_m[0, rows], w_second[pl.ds(0, cols)]) + mm(hid_m[1, rows], w_second[pl.ds(cols, cols)])
+        ).astype(BF16)
+        own_p[1, rows] = second_m[:, :BLOCK]
+        own_p[2, rows] = second_m[:, BLOCK:]
+        second.send(2 + c)
+    second.send(4)
 
     keep_m = pltpu.make_async_copy(hid_m.at[rep], out.at[main_snap], local_sem.at[5])
-    give_m = side(8, hid_m.at[rep], out.at[main_snap], out_sem.at[3], to_layer)
+    give_m = side(9, hid_m.at[rep], out.at[main_snap], out_sem.at[6], to_layer)
 
     @pl.when(layer == 0)
     def _():
@@ -336,43 +356,51 @@
     def _():
         give_m.start()
 
-    def piece_at(p, their_role):
+    def piece_at(p, rows, their_role):
         if p == 0:
-            return out.at[1, :, pl.ds(pl.multiple_of(their_role * BLOCK, BLOCK), BLOCK)]
-        return out.at[2 * their_role, :, pl.ds((p - 1) * BLOCK, BLOCK)]
-
-    put = [pltpu.make_async_copy(out_p.at[p], piece_at(p, role), local_sem.at[7 + p]) for p in range(3)]
-    push = [side(9 + p, out_p.at[p], piece_at(p, role), out_sem.at[p], to_layer) for p in range(3)]
-    take = [side(9 + p, out_p.at[p], piece_at(p, 1 - role), out_sem.at[p], to_layer) for p in range(3)]
+            return out.at[1, rows, pl.ds(pl.multiple_of(their_role * BLOCK, BLOCK), BLOCK)]
+        return out.at[2 * their_role, rows, pl.ds((p - 1) * BLOCK, BLOCK)]
+
+    put, push, take = [], [], []
+    for p in range(3):
+        for c in range(2):
+            i, src = 2 * p + c, out_p.at[p, cut_rows(c)]
+            mine, other = piece_at(p, cut_rows(c), role), piece_at(p, cut_rows(c), 1 - role)
+            put.append(pltpu.make_async_copy(src, mine, local_sem.at[7 + i]))
+            push.append(side(10 + i, src, mine, out_sem.at[i], to_layer))
+            take.append(side(10 + i, src, other, out_sem.at[i], to_layer))
 
     def finish(p):
-        gather(acc_s, parts[p], (0, 4), False)
+        own, win = own_p.at[p], win_p.at[p]
+        second.far_ready(2 * p)
+        gather(acc_s, own, win, far, depth=cut_rows(0))
+        second.far_ready(2 * p + 1)
         if p == 0:
             row = b_second[pl.ds(0, 1), share]
         else:
             row = b_second[pl.ds(0, 1), pl.ds((p - 1) * BLOCK, BLOCK)]
-        out_p[p] = (acc_s[...] + row.astype(F32)).astype(BF16)
-
-        @pl.when(layer == 1)
-        def _():
-            put[p].start()
-
-        @pl.when(layer == 0)
-        def _():
-            push[p].start()
-
-    gather(acc_s, parts[0], (1, 2, 3), True)
-    second.far_ready(0, 1)
+        for c in range(2):
+            rows = cut_rows(c)
+            gather(acc_s, own, win, far, depth=cut_rows(1), rows=rows)
+            out_p[p, rows] = (acc_s[rows] + row.astype(F32)).astype(BF16)
+
+            @pl.when(layer == 1)
+            def _():
+                put[2 * p + c].start()
+
+            @pl.when(layer == 0)
+            def _():
+                push[2 * p + c].start()
+
+    gather(acc_s, own_p.at[0], win_p.at[0], (2,) + near, True)
     finish(0)
     second.pass_on(2, 3)
     second.send(5)
-    gather(acc_s, parts[1], (1, 2, 3), True)
+    gather(acc_s, own_p.at[1], win_p.at[1], (2,) + near, True)
     second.pass_on(4)
-    second.far_ready(2, 3)
     finish(1)
     second.pass_on(5)
-    gather(acc_s, parts[2], (1, 2, 3), True)
-    second.far_ready(4, 5)
+    gather(acc_s, own_p.at[2], win_p.at[2], (2,) + near, True)
     finish(2)
 
     @pl.when(layer == 1)
@@ -389,13 +417,13 @@
     def _():
         keep_s.wait()
         keep_m.wait()
-        side(8, hid_m.at[rep], out.at[2 - main_snap], out_sem.at[3], to_layer).wait_recv()
+        side(9, hid_m.at[rep], out.at[2 - main_snap], out_sem.at[6], to_layer).wait_recv()
         for made in push:
             made.wait_send()
         for made in first_to_layer + first_to_core:
             made.wait_send()
 
-    for made in [ax_main, across, beside, relayed] + sent:
+    for made in ax_main + [across, beside, relayed] + sent:
         made.wait_send()
 
 
@@ -442,13 +470,13 @@
             pltpu.VMEM((2, 16, width), BF16),
             pltpu.VMEM((16, width), BF16),
             pltpu.VMEM((3, nodes, BLOCK), BF16),
-            pltpu.SemaphoreType.DMA((10,)),
-            pltpu.SemaphoreType.DMA((8 * CHUNKS,)),
-            pltpu.SemaphoreType.DMA((2, 2 * REACH, CHUNKS)),
+            pltpu.SemaphoreType.DMA((13,)),
+            pltpu.SemaphoreType.DMA((48,)),
+            pltpu.SemaphoreType.DMA((2, 2 * REACH, 6)),
+            pltpu.SemaphoreType.DMA((8,)),
+            pltpu.SemaphoreType.DMA((16,)),
             pltpu.SemaphoreType.DMA((6,)),
-            pltpu.SemaphoreType.DMA((12,)),
-            pltpu.SemaphoreType.DMA((6,)),
-            pltpu.SemaphoreType.DMA((4,)),
+            pltpu.SemaphoreType.DMA((7,)),
         ],
         compiler_params=pltpu.CompilerParams(
             collective_id=0, has_side_effects=True, vmem_limit_bytes=48 * 1024 * 1024

time: 80.7 us -> 77.8 us (0.964)
  Pallas kernels: 79.6 us -> 76.7 us
    pallas_call x1, Pallas kernels: 79.6 us -> 76.7 us  [per_device(): pl.pallas_call(kernel, out_shape=jax.ShapeDtypeStruct(features.shape, BF1...]
where the time goes in v3:
time: 77.8 us; the launch traced here: 77.7 us
  Pallas kernels  76.7 us (99%)
  local copies, waits for them, and re-layouts  1.02 us (1%)
    pallas_call x1, Pallas kernels, per_device(): pl.pallas_call(kernel, out_shape=jax.ShapeDtypeStruct(features.shape, BF1...  76.7 us

profile of v3, /device:TPU:8, one launch (start us, length us, event | category | flops | bytes accessed | tf_op | source)
XLA Modules:
  0.0 77.7 jit_solution(10251157359279124935)
XLA Ops:
  0.0 76.7 %shard_map.64 = bf16[3,768,256]{2,1,0:T(8,128)(2,1)S(1)} custom-call(s32[6]{0:T(128)} %counts.1, bf16[1,256]{1,0:T(2,128)(2,1)} %bias.1, s32[6,24]{1,0:T(8,128)} %tile_cols.1, bf16[3,768,256]{2,1,0:T(8,128)(2,1)} %features.1, bf16[1,512,256]{2,1,0:T(8,128)(2,1)} %weights.1, bf16[144,128,128]{2,1,0:T(8,128)(2,1)} %bitcast.3), custom_call_target="tpu_custom_call" | custom-call | tf_op jit(solution)/shard_map/pallas_call | solution.py:439
  76.7 1.0 %copy.8 = bf16[1,3,768,256]{3,2,1,0:T(8,128)(2,1)} copy(bf16[1,3,768,256]{3,2,1,0:T(8,128)(2,1)S(1)} %bitcast.2) | data formatting | bytes 2359296
